TPU v7x, 512 devices: a whole 4x8x8 slice. The times are simulated.
512 devices in a mesh: rows: 32 (over z, x), seq: 16 (over y, core).
Axes of the slice: x: 4, y: 8, z: 8, core: 2. Of those that a mesh axis runs over, the one named last changes fastest.
Arguments:
- qkv: bfloat16 [32, 1024, 3840], P('rows', 'seq'), may hold values from -24 to 24
- hidden: bfloat16 [32, 1024, 1280], P('rows', 'seq'), may hold values from -3 to 3
- segment_ids: int32 [32, 1024], P('rows', 'seq'), may hold values from 0 to 4, as said below
- key_keep: int32 [32, 1024], P('rows', 'seq'), may hold values 0 or 1
- grid_sizes: int32 [32, 4, 2], P('rows'), may hold values from 8 to 16, as said below
- owner_slots: int32 [32, 4], P('rows'), may hold values from 0 to 15, as said below
- out_weight: bfloat16 [1280, 1280], P('rows'), may hold values from -0.15625 to 0.15625
- norm_gain: float32 [1280], replicated, may hold values from 0.5 to 1.5
- norm_bias: float32 [1280], replicated, may hold values from -1.5 to 1.5
- merge_weight: bfloat16 [5120, 4096], P(None, 'seq'), may hold values from -0.078125 to 0.078125
Outputs:
- normed: bfloat16 [32, 1024, 1280], P('rows', 'seq')
- request_norm: float32 [32, 16], P('rows', 'seq')
- request_peak: float32 [32, 16], P('rows', 'seq')
Inputs may be any that keep to these rules, and one draw needn't show every extreme that they name: `segment_ids`: segment ids never fall along a pack: image j covers h_j w_j tokens right after image j - 1, and tokens after the last image carry 4; every pack ends with some such padding. Inside an image each aligned group of 4 tokens is one 2 x 2 block of the patch grid, blocks in row-major order. `grid_sizes`: both sides are even; rows run from 8 to 16, columns from 8 to 14; the first image of every pack has 16 rows and 14 columns; the images of a pack agree with segment_ids. `owner_slots`: the images of one pack have distinct slots.
All inputs are finite; a program needn't handle non-finite values. No bound on the sum of `key_keep` on one device may be relied on, other than what follows from the above.
Results may differ from a plain program's by a relative error of at most 0.0057.
Values may be sent and summed in bfloat16 or wider, within the bound.
No kernel may reach another device: no remote copies, remote signals or barrier semaphores. Data moves between devices by JAX's collectives and lax.ppermute only.
A program may use at most 64 MiB of HBM per device.

v0:
```python
import jax
import jax.numpy as jnp
from jax import lax
from jax.sharding import PartitionSpec as P

HEADS = 16
HD = 80
OUT = 4096
SLOT_DEV = 1


def positions(segment, places, patch_grid):
    image_count = patch_grid.shape[0]
    widths = patch_grid[:, 1]
    lengths = patch_grid[:, 0] * widths
    starts = jnp.cumsum(lengths) - lengths
    is_valid = segment < image_count
    image_hot = segment[:, None] == jnp.arange(image_count, dtype=jnp.int32)[None, :]
    begins = jnp.sum(jnp.where(image_hot, starts[None, :], 0), axis=1)
    token_width = jnp.maximum(jnp.sum(jnp.where(image_hot, widths[None, :], 0), axis=1), 2)
    offset = places - begins
    square = offset // 4
    corner = offset % 4
    half_width = token_width // 2
    row_pos = 2 * (square // half_width) + corner // 2
    col_pos = 2 * (square % half_width) + corner % 2
    row_pos = jnp.where(is_valid, row_pos, 0)
    col_pos = jnp.where(is_valid, col_pos, 0)
    return (row_pos, col_pos)


def rotary(values, row_pos, col_pos):
    quarter = values.shape[-1] // 4
    rates = 10000.0 ** (-jnp.arange(quarter, dtype=jnp.float32) / quarter)

    def rotate_pair(part, place):
        angle = place.astype(jnp.float32)[:, None] * rates[None, :]
        cosine = jnp.cos(angle)[:, None, :]
        sine = jnp.sin(angle)[:, None, :]
        first_half = part[..., :quarter]
        second_half = part[..., quarter:]
        return jnp.concatenate(
            [first_half * cosine - second_half * sine, second_half * cosine + first_half * sine],
            axis=-1,
        )

    middle = 2 * quarter
    return jnp.concatenate(
        [rotate_pair(values[..., :middle], row_pos), rotate_pair(values[..., middle:], col_pos)],
        axis=-1,
    )


def layer_norm(mixed, norm_gain, norm_bias):
    row_mean = jnp.mean(mixed, axis=-1, keepdims=True)
    centred = mixed - row_mean
    spread = jnp.mean(centred * centred, axis=-1, keepdims=True)
    return (centred * lax.rsqrt(spread + 1e-05) * norm_gain + norm_bias).astype(jnp.bfloat16)


def slot_counts(patch_grid, owner, slot_total):
    quads = patch_grid[:, 0] * patch_grid[:, 1] // 4
    owner_hot = owner[:, None] == jnp.arange(slot_total, dtype=jnp.int32)[None, :]
    return jnp.sum(jnp.where(owner_hot, quads[:, None], 0), axis=0)


def block_mask(segment_query, segment_keys, keep_keys, query_index, key_index, image_count):
    same_image = (
        (segment_query[:, None] == segment_keys[None, :])
        & (segment_query[:, None] < image_count)
        & (keep_keys[None, :] == 1)
    )
    return same_image | (query_index[:, None] == key_index[None, :])


def attend_dense(queries, key_rows, value_rows, segment_row, keep_row, block_rows, image_count):
    total_rows = queries.shape[1]
    key_index = jnp.arange(total_rows, dtype=jnp.int32)

    def query_block(start):
        query_part = lax.dynamic_slice_in_dim(queries, start, block_rows, 1)
        segment_part = lax.dynamic_slice_in_dim(segment_row, start, block_rows, 0)
        query_index = start + jnp.arange(block_rows, dtype=jnp.int32)
        scores = jnp.einsum(
            "hqd,hkd->hqk", query_part, key_rows, preferred_element_type=jnp.float32
        ) * HD ** (-0.5)
        allowed = block_mask(
            segment_part, segment_row, keep_row, query_index, key_index, image_count
        )[None]
        top = jnp.max(jnp.where(allowed, scores, -1e30), axis=-1, keepdims=True)
        weights = jnp.where(allowed, jnp.exp(scores - top), 0.0)
        totals = jnp.sum(weights, axis=-1, keepdims=True)
        summed = jnp.einsum(
            "hqk,hkd->hqd",
            weights.astype(jnp.bfloat16),
            value_rows,
            preferred_element_type=jnp.float32,
        )
        return (summed / totals).astype(jnp.bfloat16)

    starts = jnp.arange(total_rows // block_rows, dtype=jnp.int32) * block_rows
    blocks_out = lax.map(query_block, starts)
    return jnp.transpose(blocks_out, (1, 0, 2, 3)).reshape(queries.shape)


def body(
    qkv,
    hidden,
    segment_ids,
    key_keep,
    grid_sizes,
    owner_slots,
    out_weight,
    norm_gain,
    norm_bias,
    merge_weight,
):
    seq_count = lax.axis_size("seq")
    tok_count = qkv.shape[1]
    seq_len = tok_count * seq_count
    patch_grid = grid_sizes[0]
    image_count = patch_grid.shape[0]
    owner = owner_slots[0]
    segment = segment_ids[0]
    key_flags = key_keep[0]
    my_index = lax.axis_index("seq")
    first_token = my_index * tok_count
    places = first_token + jnp.arange(tok_count, dtype=jnp.int32)
    row_pos, col_pos = positions(segment, places, patch_grid)
    split = qkv[0].reshape(tok_count, 3, HEADS, HD)
    queries = rotary(split[:, 0].astype(jnp.float32), row_pos, col_pos).astype(jnp.bfloat16)
    key_rows = rotary(split[:, 1].astype(jnp.float32), row_pos, col_pos).astype(jnp.bfloat16)
    head_share = HEADS // seq_count
    packed = jnp.stack([queries, key_rows, split[:, 2]], axis=1).reshape(
        tok_count, 3, seq_count, head_share, HD
    )
    segment_tile = jnp.broadcast_to(
        segment[:, None, None, None, None], (tok_count, 1, seq_count, head_share, 1)
    )
    keep_tile = jnp.broadcast_to(
        key_flags[:, None, None, None, None], (tok_count, 1, seq_count, head_share, 1)
    )
    block_rows = 512
    while seq_len % block_rows:
        block_rows = block_rows // 2
    tile_rows = 128
    while seq_len % tile_rows:
        tile_rows = tile_rows // 2
    packed_all = lax.all_to_all(packed, "seq", split_axis=2, concat_axis=0, tiled=True)
    segment_all = lax.all_to_all(segment_tile, "seq", split_axis=2, concat_axis=0, tiled=True)
    keep_all = lax.all_to_all(keep_tile, "seq", split_axis=2, concat_axis=0, tiled=True)
    segment_row = segment_all[:, 0, 0, 0, 0]
    keep_row = keep_all[:, 0, 0, 0, 0]
    head_queries = jnp.transpose(packed_all[:, 0, 0], (1, 0, 2))
    head_keys = jnp.transpose(packed_all[:, 1, 0], (1, 0, 2))
    head_values = jnp.transpose(packed_all[:, 2, 0], (1, 0, 2))
    result = attend_dense(
        head_queries, head_keys, head_values, segment_row, keep_row, block_rows, image_count
    )
    head_out = jnp.transpose(result, (1, 0, 2))
    token_out = lax.all_to_all(head_out, "seq", split_axis=0, concat_axis=1, tiled=True)
    attended = token_out.reshape(tok_count, HEADS * HD)
    mixed_part = jnp.dot(
        attended,
        lax.all_gather(out_weight, "rows", axis=0, tiled=True),
        preferred_element_type=jnp.float32,
    )
    mixed = hidden[0].astype(jnp.float32) + mixed_part
    normed = layer_norm(mixed, norm_gain, norm_bias)
    merged = normed.reshape(tok_count // 4, 4 * normed.shape[1])
    projected = jnp.dot(
        lax.all_gather(merged, "seq", axis=0, tiled=True),
        merge_weight,
        preferred_element_type=jnp.float32,
    )
    merge_stats = jnp.stack([jnp.sum(projected * projected, axis=1), jnp.max(projected, axis=1)])
    slot_total = SLOT_DEV * seq_count
    lengths = patch_grid[:, 0] * patch_grid[:, 1]
    ends = jnp.cumsum(lengths)
    merge_first = 4 * jnp.arange(seq_len // 4, dtype=jnp.int32)
    merge_image = jnp.sum((merge_first[:, None] >= ends[None, :]).astype(jnp.int32), axis=1)
    is_valid = merge_image < image_count
    image_hot = merge_image[:, None] == jnp.arange(image_count, dtype=jnp.int32)[None, :]
    merge_slot = jnp.sum(jnp.where(image_hot, owner[None, :], 0), axis=1)
    slot_hot = (merge_slot[:, None] == jnp.arange(slot_total, dtype=jnp.int32)[None, :]) & is_valid[
        :, None
    ]
    sums_all = jnp.sum(jnp.where(slot_hot, merge_stats[0][:, None], 0.0), axis=0)
    tops_all = jnp.max(jnp.where(slot_hot, merge_stats[1][:, None], -1e30), axis=0)
    own_first = my_index * SLOT_DEV
    slot_sums = lax.psum_scatter(sums_all, "seq", scatter_dimension=0, tiled=True)
    slot_tops = lax.dynamic_slice_in_dim(lax.pmax(tops_all, "seq"), own_first, SLOT_DEV)
    counts = lax.dynamic_slice_in_dim(
        slot_counts(patch_grid, owner, slot_total), own_first, SLOT_DEV
    )
    present = counts > 0
    divisor = (jnp.maximum(counts, 1) * OUT).astype(jnp.float32)
    norm_out = jnp.where(present, jnp.sqrt(slot_sums / divisor + 1e-06), 0.0)
    peak_out = jnp.where(present, slot_tops, 0.0)
    return (normed[None], norm_out[None], peak_out[None])


def solution(mesh):
    placed = (
        P("rows", "seq", None),
        P("rows", "seq", None),
        P("rows", "seq"),
        P("rows", "seq"),
        P("rows", None, None),
        P("rows", None),
        P("rows", None),
        P(),
        P(),
        P(None, "seq"),
    )
    return jax.shard_map(
        body,
        mesh=mesh,
        in_specs=placed,
        out_specs=(P("rows", "seq", None), P("rows", "seq"), P("rows", "seq")),
        check_vma=False,
    )
```

profile of v0, /device:TPU:1, one launch (start us, length us, event | category | flops | bytes accessed | tf_op | source)
XLA Modules:
  0.0 224.3 jit_solution(8085196978204176360)
XLA Ops:
  7.2 1.4 broadcast_in_dim.146
  8.6 10.1 %all-to-all-start = ((s32[64,1,16,1,1]{0,4,3,1,2:T(1,128)}), s32[64,1,16,1,1]{0,4,3,1,2:T(1,128)S(1)}, u32[]{:S(2)}, u32[]{:S(2)}) async-start(s32[64,1,16,1,1]{0,4,3,1,2:T(1,128)} %broadcast_in_dim.146), calls=%async_computation | async-start | bytes 16384 | tf_op jit(solution)/shard_map/all_to_all | solution.py:150
  19.4 2.4 %reshape_squeeze.3 = bf16[64,3,16,80]{3,2,1,0:T(8,128)(2,1)S(1)} reshape(bf16[1,64,3840]{2,1,0:T(8,128)(2,1)} %param.12) | data formatting | bytes 983040 | tf_op jit(solution)/shard_map/reshape;squeeze | solution.py:130
  30.8 7.3 %all-to-all-start.1 = ((s32[64,1,16,1,1]{0,4,3,1,2:T(1,128)}), s32[64,1,16,1,1]{0,4,3,1,2:T(1,128)S(1)}, u32[]{:S(2)}, u32[]{:S(2)}) async-start(s32[64,1,16,1,1]{0,4,3,1,2:T(1,128)} %broadcast_in_dim.148), calls=%async_computation.1 | async-start | bytes 16384 | tf_op jit(solution)/shard_map/all_to_all | solution.py:151
  38.1 1.5 maximum_bitcast_fusion
  40.7 4.3 %all-to-all-done.1 = s32[64,1,16,1,1]{0,4,3,1,2:T(1,128)S(1)} async-done(((s32[64,1,16,1,1]{0,4,3,1,2:T(1,128)}), s32[64,1,16,1,1]{0,4,3,1,2:T(1,128)S(1)}, u32[]{:S(2)}, u32[]{:S(2)}) %all-to-all-start.1) | async-done | bytes 4128 | tf_op jit(solution)/shard_map/all_to_all | solution.py:151
  45.0 4.1 %all-to-all-start.2 = ((bf16[64,3,16,1,80]{4,0,1,3,2:T(8,128)(2,1)}), bf16[64,3,16,1,80]{4,0,1,3,2:T(8,128)(2,1)S(1)}, u32[]{:S(2)}, u32[]{:S(2)}) async-start(bf16[64,3,16,1,80]{4,0,1,3,2:T(8,128)(2,1)} %copy.49), calls=%async_computation.2 | async-start | bytes 1572864 | tf_op jit(solution)/shard_map/all_to_all | solution.py:149
  49.9 22.0 %all-to-all-done.2 = bf16[64,3,16,1,80]{4,0,1,3,2:T(8,128)(2,1)S(1)} async-done(((bf16[64,3,16,1,80]{4,0,1,3,2:T(8,128)(2,1)}), bf16[64,3,16,1,80]{4,0,1,3,2:T(8,128)(2,1)S(1)}, u32[]{:S(2)}, u32[]{:S(2)}) %all-to-all-start.2) | async-done | bytes 491552 | tf_op jit(solution)/shard_map/all_to_all | solution.py:149
  71.9 1.4 copy.50
  73.3 1.9 all_to_all.61
  76.2 20.3 %while.11 = (s32[]{:T(128)}, bf16[2,1,512,80]{2,3,1,0:T(8,128)(2,1)}, s32[2]{0:T(128)}, s32[1024]{0:T(1024)S(1)}, s32[1024,1,1,1,1]{0,4,3,2,1:T(1,128)S(1)}, /*i...) while((s32[]{:T(128)}, ...), condition=%wide.region_6.7_spmd.clone, body=%wide.region_3.6_spmd.clone.sunk | while | flops 181486592 | bytes 8243435 | solution.py:102
  80.4 2.2 select_reduce_fusion.8
  82.6 1.5 fusion.49
  84.1 1.6 fusion.50
  90.6 2.2 select_reduce_fusion.8
  92.8 1.5 fusion.49
  94.3 1.6 fusion.50
  98.3 2.3 %reduce.6 = bf16[1024,80]{1,0:T(8,128)(2,1)S(1)} reduce(bf16[1024,1,80]{2,1,0:T(2,128)(2,1)S(1)} %reshape.474, bf16[]{:T(256)} %broadcast.483), dimensions={1}, to_apply=%reshape.474.reduce_sub_computation | reduce | bytes 327682 | tf_op jit(solution)/shard_map/transpose;reshape;transpose | solution.py:160
  101.0 12.5 %all_to_all.69 = bf16[16,2,2560]{2,1,0:T(2,128)(2,1)S(1)} all-to-all(bf16[16,2,2560]{2,1,0:T(2,128)(2,1)S(1)} %reshape.477), channel_id=1, replica_groups=mesh['rows'=32,'seq'=16] {'seq'}, dimensions={0} | all-to-all | bytes 327680 | tf_op jit(solution)/shard_map/all_to_all | solution.py:161
  115.5 2.7 %fusion.37 = (f32[64]{0:T(128)S(1)}, f32[64,1280]{1,0:T(8,128)S(1)}) fusion(bf16[64,1280]{1,0:T(8,128)(2,1)S(1)} %reshape.466, bf16[1280,1280]{1,0:T(8,128)(2,1)} %all-gather.3.cloned.1.call-done, bf16[1,64,1280]{2,1,0:T(8,128)(2,1)S(1)} %copy-done.1), kind=kOutput, calls=%fused_computation.105 | convolution fusion | flops 209960896 | bytes 3932416 | tf_op jit(solution)/shard_map/dot_general | solution.py:163
  123.7 36.8 %all-gather.5.cloned.1.call-done = bf16[256,5120]{1,0:T(8,128)(2,1)} async-done(((bf16[16,5120]{1,0:T(8,128)(2,1)}), bf16[256,5120]{1,0:T(8,128)(2,1)}) %all-gather.5.cloned.1.call-update) | async-done | bytes 2621456 | tf_op jit(solution)/shard_map/all_gather | solution.py:172
  160.5 2.9 %fusion.36 = (f32[256]{0:T(256)S(1)}, f32[256]{0:T(256)S(1)}) fusion(bf16[256,5120]{1,0:T(8,128)(2,1)} %all-gather.5.cloned.1.call-done, bf16[5120,256]{1,0:T(8,128)(2,1)S(1)} %copy-done), kind=kOutput, calls=%fused_computation.104 | convolution fusion | flops 671284736 | bytes 5244928 | tf_op jit(solution)/shard_map/dot_general | solution.py:171
  163.5 23.2 %pmax.7 = f32[16]{0:T(128)S(1)} all-reduce(f32[16]{0:T(128)S(1)} %get-tuple-element.96), channel_id=1, replica_groups=mesh['rows'=32,'seq'=16] {'seq'}, use_global_device_ids=true, to_apply=%region_17.18 | all-reduce | flops 16 | bytes 128 | tf_op jit(solution)/shard_map/pmax | solution.py:192
  187.4 25.2 %all-reduce = f32[16]{0:T(128)S(1)} all-reduce(f32[16]{0:T(128)S(1)} %get-tuple-element.97), channel_id=2, replica_groups=mesh['rows'=32,'seq'=16] {'seq'}, use_global_device_ids=true, to_apply=%region_14.15.clone | all-reduce | flops 16 | bytes 128
  (83 shorter events, 28.3 us)
Async XLA Ops:
  7.2 153.3 %copy-start = (bf16[5120,256]{1,0:T(8,128)(2,1)S(1)}, bf16[5120,256]{1,0:T(8,128)(2,1)}, u32[]{:S(2)}) copy-start(bf16[5120,256]{1,0:T(8,128)(2,1)} %param.21) | copy-start | bytes 7864324
  8.6 21.6 %all-to-all-start = ((s32[64,1,16,1,1]{0,4,3,1,2:T(1,128)}), s32[64,1,16,1,1]{0,4,3,1,2:T(1,128)S(1)}, u32[]{:S(2)}, u32[]{:S(2)}) async-start(s32[64,1,16,1,1]{0,4,3,1,2:T(1,128)} %broadcast_in_dim.146), calls=%async_computation | async-start | bytes 16384 | tf_op jit(solution)/shard_map/all_to_all | solution.py:150
  18.7 96.8 %all-gather.3.cloned.1.call-start = ((), (), s32[]{:S(2)}) async-start(), calls=%async_computation.4 | async-start | bytes 3379200 | tf_op jit(solution)/shard_map/all_gather | solution.py:165
  28.0 2.2 copy-start.6
  30.8 14.2 %all-to-all-start.1 = ((s32[64,1,16,1,1]{0,4,3,1,2:T(1,128)}), s32[64,1,16,1,1]{0,4,3,1,2:T(1,128)S(1)}, u32[]{:S(2)}, u32[]{:S(2)}) async-start(s32[64,1,16,1,1]{0,4,3,1,2:T(1,128)} %broadcast_in_dim.148), calls=%async_computation.1 | async-start | bytes 16384 | tf_op jit(solution)/shard_map/all_to_all | solution.py:151
  45.0 26.8 %all-to-all-start.2 = ((bf16[64,3,16,1,80]{4,0,1,3,2:T(8,128)(2,1)}), bf16[64,3,16,1,80]{4,0,1,3,2:T(8,128)(2,1)S(1)}, u32[]{:S(2)}, u32[]{:S(2)}) async-start(bf16[64,3,16,1,80]{4,0,1,3,2:T(8,128)(2,1)} %copy.49), calls=%async_computation.2 | async-start | bytes 1572864 | tf_op jit(solution)/shard_map/all_to_all | solution.py:149
  49.1 111.4 %all-gather.5.cloned.1.call-start = ((), (), s32[]{:S(2)}) async-start(), calls=%async_computation.5 | async-start | bytes 2785280 | tf_op jit(solution)/shard_map/all_gather | solution.py:172
  82.6 1.5 copy-start.2
  85.7 0.7 copy-start.3
  92.8 1.5 copy-start.2
  95.8 0.7 copy-start.3
  101.0 14.5 %copy-start.1 = (bf16[1,64,1280]{2,1,0:T(8,128)(2,1)S(1)}, bf16[1,64,1280]{2,1,0:T(8,128)(2,1)}, u32[]{:S(2)}) copy-start(bf16[1,64,1280]{2,1,0:T(8,128)(2,1)} %param.13) | copy-start | bytes 491524
  115.4 3.0 %copy-start.4 = (f32[1280]{0:T(1024)S(1)}, f32[1280]{0:T(1024)}, u32[]{:S(2)}) copy-start(f32[1280]{0:T(1024)} %param.20) | copy-start | bytes 15364
  115.4 3.0 %copy-start.5 = (f32[1280]{0:T(1024)S(1)}, f32[1280]{0:T(1024)}, u32[]{:S(2)}) copy-start(f32[1280]{0:T(1024)} %param.19) | copy-start | bytes 15364
  115.5 4.0 %copy-start.7 = (s32[1,4]{1,0:T(1,128)S(1)}, s32[1,4]{1,0:T(1,128)}, u32[]{:S(2)}) copy-start(s32[1,4]{1,0:T(1,128)} %param.17) | copy-start | bytes 52
  115.5 4.0 %copy-start.8 = (s32[4]{0:T(128)S(1)}, s32[4]{0:T(128)}, u32[]{:S(2)}) copy-start(s32[4]{0:T(128)} %get-tuple-element.120) | copy-start | bytes 52
Sparse Core Ops, SparseCore 0:
  22.7 84.2 all-gather.2
  119.5 40.9 all-gather.4
where the time goes:
time: 225 us; the launch traced here: 224 us
  waiting for transfers between devices  63.9 us (28%)
  blocking collectives  61 us (27%)
  local copies, waits for them, and re-layouts  22.6 us (10%)
  starting transfers between devices  21.5 us (10%)
  between operations  19.3 us (9%)
  other arithmetic  18.7 us (8%)
  matrix products  13.1 us (6%)
  loops' own time  4.26 us (2%)
    all_gather x1, waiting for transfers between devices, body(): lax.all_gather(merged, 'seq', axis=0, tiled=True)  36.8 us
    unnamed x1, blocking collectives  25.2 us
    pmax x1, blocking collectives, body(): lax.pmax(tops_all, 'seq')  23.2 us
    all_to_all x1, waiting for transfers between devices, body(): lax.all_to_all(packed, 'seq', split_axis=2, concat_axis=0, tiled=True)  22 us
    all_to_all x1, blocking collectives, body(): lax.all_to_all(head_out, 'seq', split_axis=0, concat_axis=1, tiled=True)  12.5 us
    all_to_all x1, starting transfers between devices, body(): lax.all_to_all(segment_tile, 'seq', split_axis=2, concat_axis=0, tiled=True)  10.1 us
    all_to_all x1, starting transfers between devices, body(): lax.all_to_all(keep_tile, 'seq', split_axis=2, concat_axis=0, tiled=True)  7.27 us
  transfers between devices with their start and end apart: 5, of which 3 were waited for; matrix products, arithmetic and copies ran while one was open for 18% of the time, Pallas kernels for 0%

commit v1 on v0

--- a/solution.py
+++ b/solution.py
@@ -169,7 +169,9 @@
     normed = layer_norm(mixed, norm_gain, norm_bias)
     merged = normed.reshape(tok_count // 4, 4 * normed.shape[1])
     projected = jnp.dot(
-        lax.all_gather(merged, "seq", axis=0, tiled=True),
+        jnp.concatenate(
+            lax.all_to_all(jnp.stack([merged] * lax.axis_size("seq")), "seq", 0, 0), axis=0
+        ),
         merge_weight,
         preferred_element_type=jnp.float32,
     )

time: 225 us -> 248 us (1.10)
  waiting for transfers between devices: 63.9 us -> 83 us
  starting transfers between devices: 21.5 us -> 25.9 us
    all_to_all x0 -> x1, waiting for transfers between devices: none -> 55.4 us  [body(): lax.all_to_all(jnp.stack([merged] * lax.axis_size('seq')), 'seq', 0, 0)]
    all_gather x1 -> x0, waiting for transfers between devices: 36.8 us -> none  [body(): lax.all_gather(merged, 'seq', axis=0, tiled=True)]
    all_to_all x0 -> x1, starting transfers between devices: none -> 4.48 us  [body(): lax.all_to_all(jnp.stack([merged] * lax.axis_size('seq')), 'seq', 0, 0)]
  transfers between devices with their start and end apart: 5 -> 5, of which waited for: 3 -> 3; matrix products, arithmetic and copies ran while one was open for 18% -> 16% of each run, Pallas kernels for 0% -> 0%
where the time goes in v1:
time: 248 us; the launch traced here: 247 us
  waiting for transfers between devices  83 us (33%)
  blocking collectives  60.5 us (24%)
  starting transfers between devices  25.9 us (10%)
  local copies, waits for them, and re-layouts  22.4 us (9%)
  between operations  19.2 us (8%)
  other arithmetic  18.2 us (7%)
  matrix products  13.2 us (5%)
  loops' own time  4.25 us (2%)
    all_to_all x1, waiting for transfers between devices, body(): lax.all_to_all(jnp.stack([merged] * lax.axis_size('seq')), 'seq', 0, 0)  55.4 us
    pmax x1, blocking collectives, body(): lax.pmax(tops_all, 'seq')  24.1 us
    unnamed x1, blocking collectives  23.9 us
    all_to_all x1, waiting for transfers between devices, body(): lax.all_to_all(packed, 'seq', split_axis=2, concat_axis=0, tiled=True)  22.5 us
    all_to_all x1, blocking collectives, body(): lax.all_to_all(head_out, 'seq', split_axis=0, concat_axis=1, tiled=True)  12.5 us
    all_to_all x1, starting transfers between devices, body(): lax.all_to_all(segment_tile, 'seq', split_axis=2, concat_axis=0, tiled=True)  10.1 us
    all_to_all x1, starting transfers between devices, body(): lax.all_to_all(keep_tile, 'seq', split_axis=2, concat_axis=0, tiled=True)  7.27 us
  transfers between devices with their start and end apart: 5, of which 3 were waited for; matrix products, arithmetic and copies ran while one was open for 16% of the time, Pallas kernels for 0%

profile of v1, /device:TPU:1, one launch (start us, length us, event | category | flops | bytes accessed | tf_op | source)
XLA Modules:
  0.0 246.7 jit_solution(313945075450464884)
XLA Ops:
  8.6 10.1 %all-to-all-start = ((s32[64,1,16,1,1]{0,4,3,1,2:T(1,128)}), s32[64,1,16,1,1]{0,4,3,1,2:T(1,128)S(1)}, u32[]{:S(2)}, u32[]{:S(2)}) async-start(s32[64,1,16,1,1]{0,4,3,1,2:T(1,128)} %broadcast_in_dim.146), calls=%async_computation | async-start | bytes 16384 | tf_op jit(solution)/shard_map/all_to_all | solution.py:150
  19.4 2.4 reshape_squeeze.3
  30.8 7.3 %all-to-all-start.1 = ((s32[64,1,16,1,1]{0,4,3,1,2:T(1,128)}), s32[64,1,16,1,1]{0,4,3,1,2:T(1,128)S(1)}, u32[]{:S(2)}, u32[]{:S(2)}) async-start(s32[64,1,16,1,1]{0,4,3,1,2:T(1,128)} %broadcast_in_dim.148), calls=%async_computation.1 | async-start | bytes 16384 | tf_op jit(solution)/shard_map/all_to_all | solution.py:151
  38.1 1.5 maximum_bitcast_fusion
  40.7 4.3 %all-to-all-done.1 = s32[64,1,16,1,1]{0,4,3,1,2:T(1,128)S(1)} async-done(((s32[64,1,16,1,1]{0,4,3,1,2:T(1,128)}), s32[64,1,16,1,1]{0,4,3,1,2:T(1,128)S(1)}, u32[]{:S(2)}, u32[]{:S(2)}) %all-to-all-start.1) | async-done | bytes 4128 | tf_op jit(solution)/shard_map/all_to_all | solution.py:151
  45.0 4.1 %all-to-all-start.2 = ((bf16[64,3,16,1,80]{4,0,1,3,2:T(8,128)(2,1)}), bf16[64,3,16,1,80]{4,0,1,3,2:T(8,128)(2,1)S(1)}, u32[]{:S(2)}, u32[]{:S(2)}) async-start(bf16[64,3,16,1,80]{4,0,1,3,2:T(8,128)(2,1)} %copy.49), calls=%async_computation.2 | async-start | bytes 1572864 | tf_op jit(solution)/shard_map/all_to_all | solution.py:149
  49.3 22.5 %all-to-all-done.2 = bf16[64,3,16,1,80]{4,0,1,3,2:T(8,128)(2,1)S(1)} async-done(((bf16[64,3,16,1,80]{4,0,1,3,2:T(8,128)(2,1)}), bf16[64,3,16,1,80]{4,0,1,3,2:T(8,128)(2,1)S(1)}, u32[]{:S(2)}, u32[]{:S(2)}) %all-to-all-start.2) | async-done | bytes 491552 | tf_op jit(solution)/shard_map/all_to_all | solution.py:149
  73.3 1.9 all_to_all.64
  76.2 19.0 %while.11 = (s32[]{:T(128)}, bf16[2,1,512,80]{2,3,1,0:T(8,128)(2,1)}, s32[2]{0:T(128)S(1)}, s32[1024]{0:T(1024)S(1)}, s32[1024,1,1,1,1]{0,4,3,2,1:T(1,128)S(1)},...) while((s32[]{:T(128)}, ...), condition=%wide.region_6.7_spmd.clone, body=%wide.region_3.6_spmd.clone.sunk | while | flops 181486592 | bytes 8243443 | solution.py:102
  79.8 2.2 select_reduce_fusion.8
  82.0 1.5 fusion.49
  83.5 1.6 fusion.50
  89.3 2.2 select_reduce_fusion.8
  91.5 1.5 fusion.49
  93.0 1.6 fusion.50
  97.0 2.3 reduce.6
  99.8 12.5 %all_to_all.74 = bf16[16,2,2560]{2,1,0:T(2,128)(2,1)S(1)} all-to-all(bf16[16,2,2560]{2,1,0:T(2,128)(2,1)S(1)} %reshape.479), channel_id=1, replica_groups=mesh['rows'=32,'seq'=16] {'seq'}, dimensions={0} | all-to-all | bytes 327680 | tf_op jit(solution)/shard_map/all_to_all | solution.py:161
  114.2 2.7 %fusion.37 = (f32[64]{0:T(128)S(1)}, f32[64,1280]{1,0:T(8,128)S(1)}) fusion(bf16[64,1280]{1,0:T(8,128)(2,1)S(1)} %reshape.468, bf16[1280,1280]{1,0:T(8,128)(2,1)} %all-gather.2.cloned.1.call-done, bf16[1,64,1280]{2,1,0:T(8,128)(2,1)S(1)} %copy-done.1), kind=kOutput, calls=%fused_computation.105 | convolution fusion | flops 209960896 | bytes 3932416 | tf_op jit(solution)/shard_map/dot_general | solution.py:163
  117.4 1.8 stack.9
  119.2 4.5 %all-to-all-start.4 = ((bf16[16,16,5120]{2,1,0:T(8,128)(2,1)}), bf16[16,16,5120]{2,1,0:T(8,128)(2,1)}, u32[]{:S(2)}, u32[]{:S(2)}) async-start(bf16[16,16,5120]{2,1,0:T(8,128)(2,1)} %stack.9), calls=%async_computation.4 | async-start | bytes 5242880 | tf_op jit(solution)/shard_map/all_to_all | solution.py:173
  128.0 55.4 %all-to-all-done.4 = bf16[16,16,5120]{2,1,0:T(8,128)(2,1)} async-done(((bf16[16,16,5120]{2,1,0:T(8,128)(2,1)}), bf16[16,16,5120]{2,1,0:T(8,128)(2,1)}, u32[]{:S(2)}, u32[]{:S(2)}) %all-to-all-start.4) | async-done | bytes 2621472 | tf_op jit(solution)/shard_map/all_to_all | solution.py:173
  183.4 2.9 %fusion.36 = (f32[256]{0:T(256)S(1)}, f32[256]{0:T(256)S(1)}) fusion(bf16[256,5120]{1,0:T(8,128)(2,1)} %bitcast.38, bf16[5120,256]{1,0:T(8,128)(2,1)S(1)} %copy-done), kind=kOutput, calls=%fused_computation.104 | convolution fusion | flops 671284736 | bytes 5244928 | tf_op jit(solution)/shard_map/dot_general | solution.py:171
  186.4 23.9 %all-reduce = f32[16]{0:T(128)S(1)} all-reduce(f32[16]{0:T(128)S(1)} %get-tuple-element.97), channel_id=2, replica_groups=mesh['rows'=32,'seq'=16] {'seq'}, use_global_device_ids=true, to_apply=%region_14.15.clone | all-reduce | flops 16 | bytes 128
  212.3 24.1 %pmax.7 = f32[16]{0:T(128)S(1)} all-reduce(f32[16]{0:T(128)S(1)} %get-tuple-element.96), channel_id=1, replica_groups=mesh['rows'=32,'seq'=16] {'seq'}, use_global_device_ids=true, to_apply=%region_17.18 | all-reduce | flops 16 | bytes 128 | tf_op jit(solution)/shard_map/pmax | solution.py:194
  (87 shorter events, 28.5 us)
Async XLA Ops:
  7.2 176.2 %copy-start = (bf16[5120,256]{1,0:T(8,128)(2,1)S(1)}, bf16[5120,256]{1,0:T(8,128)(2,1)}, u32[]{:S(2)}) copy-start(bf16[5120,256]{1,0:T(8,128)(2,1)} %param.21) | copy-start | bytes 7864324
  8.6 21.6 %all-to-all-start = ((s32[64,1,16,1,1]{0,4,3,1,2:T(1,128)}), s32[64,1,16,1,1]{0,4,3,1,2:T(1,128)S(1)}, u32[]{:S(2)}, u32[]{:S(2)}) async-start(s32[64,1,16,1,1]{0,4,3,1,2:T(1,128)} %broadcast_in_dim.146), calls=%async_computation | async-start | bytes 16384 | tf_op jit(solution)/shard_map/all_to_all | solution.py:150
  18.7 95.5 %all-gather.2.cloned.1.call-start = ((), (), s32[]{:S(2)}) async-start(), calls=%async_computation.5 | async-start | bytes 3379200 | tf_op jit(solution)/shard_map/all_gather | solution.py:165
  23.3 5.4 %copy-start.6 = (s32[4,1]{0,1:T(1,128)}, s32[4,1]{0,1:T(1,128)S(1)}, u32[]{:S(2)}) copy-start(s32[4,1]{0,1:T(1,128)S(1)} %reduce-window.7) | copy-start | bytes 52
  28.7 1.5 copy-start.8
  30.8 14.2 %all-to-all-start.1 = ((s32[64,1,16,1,1]{0,4,3,1,2:T(1,128)}), s32[64,1,16,1,1]{0,4,3,1,2:T(1,128)S(1)}, u32[]{:S(2)}, u32[]{:S(2)}) async-start(s32[64,1,16,1,1]{0,4,3,1,2:T(1,128)} %broadcast_in_dim.148), calls=%async_computation.1 | async-start | bytes 16384 | tf_op jit(solution)/shard_map/all_to_all | solution.py:151
  45.0 26.8 %all-to-all-start.2 = ((bf16[64,3,16,1,80]{4,0,1,3,2:T(8,128)(2,1)}), bf16[64,3,16,1,80]{4,0,1,3,2:T(8,128)(2,1)S(1)}, u32[]{:S(2)}, u32[]{:S(2)}) async-start(bf16[64,3,16,1,80]{4,0,1,3,2:T(8,128)(2,1)} %copy.49), calls=%async_computation.2 | async-start | bytes 1572864 | tf_op jit(solution)/shard_map/all_to_all | solution.py:149
  82.0 1.5 copy-start.2
  85.1 0.7 copy-start.3
  91.5 1.5 copy-start.2
  94.6 0.7 copy-start.3
  99.7 14.4 %copy-start.1 = (bf16[1,64,1280]{2,1,0:T(8,128)(2,1)S(1)}, bf16[1,64,1280]{2,1,0:T(8,128)(2,1)}, u32[]{:S(2)}) copy-start(bf16[1,64,1280]{2,1,0:T(8,128)(2,1)} %param.13) | copy-start | bytes 491524
  114.1 3.0 %copy-start.4 = (f32[1280]{0:T(1024)S(1)}, f32[1280]{0:T(1024)}, u32[]{:S(2)}) copy-start(f32[1280]{0:T(1024)} %param.20) | copy-start | bytes 15364
  114.1 3.0 %copy-start.5 = (f32[1280]{0:T(1024)S(1)}, f32[1280]{0:T(1024)}, u32[]{:S(2)}) copy-start(f32[1280]{0:T(1024)} %param.19) | copy-start | bytes 15364
  119.2 4.5 %copy-start.9 = (s32[1,4]{1,0:T(1,128)S(1)}, s32[1,4]{1,0:T(1,128)}, u32[]{:S(2)}) copy-start(s32[1,4]{1,0:T(1,128)} %param.17) | copy-start | bytes 52
  119.2 4.5 %copy-start.10 = (s32[4]{0:T(128)S(1)}, s32[4]{0:T(128)}, u32[]{:S(2)}) copy-start(s32[4]{0:T(128)} %get-tuple-element.120) | copy-start | bytes 52
  119.2 7.8 %copy-start.7 = (s32[4,1]{0,1:T(1,128)S(1)}, s32[4,1]{0,1:T(1,128)}, u32[]{:S(2)}) copy-start(s32[4,1]{0,1:T(1,128)} %copy-done.6) | copy-start | bytes 52
  119.2 64.2 %all-to-all-start.4 = ((bf16[16,16,5120]{2,1,0:T(8,128)(2,1)}), bf16[16,16,5120]{2,1,0:T(8,128)(2,1)}, u32[]{:S(2)}, u32[]{:S(2)}) async-start(bf16[16,16,5120]{2,1,0:T(8,128)(2,1)} %stack.9), calls=%async_computation.4 | async-start | bytes 5242880 | tf_op jit(solution)/shard_map/all_to_all | solution.py:173
Sparse Core Ops, SparseCore 0:
  22.7 84.2 all-gather.1
